TPU v7x, 32 devices: a whole 2x2x4 slice. The times are simulated.
32 devices in a mesh: heads: 2 (over y), ctx: 16 (over z, x, core).
Axes of the slice: x: 2, y: 2, z: 4, core: 2. Of those that a mesh axis runs over, the one named last changes fastest.
Arguments:
- queries: bfloat16 [8, 4096, 128], P('heads', 'ctx'), may hold values from -6 to 6
- key_rows: bfloat16 [8, 4096, 128], P('heads', 'ctx'), may hold values from -6 to 6
- value_rows: bfloat16 [8, 4096, 128], P('heads', 'ctx'), may hold values from -6 to 6
- level_weights: float32 [8, 13, 4096], P('heads', None, 'ctx'), may hold values from 0.1 to 3
- norm_gain: float32 [8, 128], P('heads'), may hold values from 0.1 to 1.9
- grad_normed: bfloat16 [8, 4096, 128], P('heads', 'ctx'), may hold values from -6 to 6
Outputs:
- normed: bfloat16 [8, 4096, 128], P('heads', 'ctx')
- grad_queries: bfloat16 [8, 4096, 128], P('heads', 'ctx')
- grad_keys: bfloat16 [8, 4096, 128], P('heads', 'ctx')
- grad_values: bfloat16 [8, 4096, 128], P('heads', 'ctx')
- grad_level_weights: float32 [8, 13, 4096], P('heads', None, 'ctx')
All inputs are finite; a program needn't handle non-finite values.
Results may differ from a plain program's by a relative error of at most 0.006.
Values sent between devices are 32-bit elements; how exact they have to be, the bound alone decides.
A program may use at most 64 MiB of HBM per device.

v0:
```python
import math

import jax
import jax.numpy as jnp
from jax import lax
from jax.sharding import PartitionSpec as P

EPS = 1e-06
HIGH = lax.Precision.HIGHEST


def from_partner(value, axis, bit):
    mask = 2**bit
    pairs = [(source, source ^ mask) for source in range(lax.axis_size(axis))]
    return lax.ppermute(value, axis, pairs)


def level_scale(number, head_dim):
    return 2.0 ** (-max(number - 1, 0) / 2.0) / math.sqrt(head_dim)


def level_matrix(count):
    position = jnp.arange(count, dtype=jnp.int32)
    differ = jnp.bitwise_xor(position[:, None], position[None, :])
    bucket = jnp.zeros((count, count), jnp.int32)
    for exponent in range(count.bit_length() - 1):
        bucket = bucket + (differ >= 2**exponent).astype(jnp.int32)
    causal = position[None, :] <= position[:, None]
    return (bucket, causal)


def near_weights(factors, bucket, causal, head_dim):
    weights = jnp.zeros(factors[0].shape + (bucket.shape[1],), jnp.float32)
    for number in range(len(factors)):
        scaled = factors[number] * level_scale(number, head_dim)
        weights = weights + jnp.where(
            (bucket == number) & causal, scaled[..., None], jnp.float32(0.0)
        )
    return weights


def pair_level(matrix, step_bit):
    return from_partner(matrix, "ctx", step_bit)


def shards(queries, key_rows, value_rows, level_weights, norm_gain, grad_normed):
    heads_here, tokens_here, head_dim = queries.shape
    local_levels = tokens_here.bit_length()
    far_levels = lax.axis_size("ctx").bit_length() - 1
    block_index = lax.axis_index("ctx")
    width = heads_here * lax.axis_size("heads") * head_dim
    key_value = jnp.einsum("hsd,hse->hde", key_rows, value_rows, preferred_element_type=jnp.float32)
    group_sum = key_value
    far_list = []
    for step_bit in range(far_levels):
        partner = from_partner(group_sum, "ctx", step_bit)
        bit_set = block_index >> step_bit & 1
        far_list.append(jnp.where(bit_set == 1, partner, jnp.float32(0.0)))
        group_sum = group_sum + partner
    states = jnp.stack(far_list, 0)
    bucket, causal = level_matrix(tokens_here)
    weights = near_weights(
        [level_weights[:, number, :] for number in range(local_levels)], bucket, causal, head_dim
    )
    scores = jnp.einsum("htd,hsd->hts", queries, key_rows, preferred_element_type=jnp.float32)
    weighted = (weights * scores).astype(jnp.bfloat16)
    near_out = jnp.einsum("hts,hse->hte", weighted, value_rows, preferred_element_type=jnp.float32)
    far_scale = jnp.stack(
        [
            level_weights[:, local_levels + depth, :] * level_scale(local_levels + depth, head_dim)
            for depth in range(far_levels)
        ],
        0,
    )
    query_wide = queries.astype(jnp.float32)
    far_terms = jnp.einsum("htd,mhde->mhte", query_wide, states, precision=HIGH)
    attended = near_out + jnp.sum(far_scale[..., None] * far_terms, 0)
    totals = lax.psum(jnp.sum(attended * attended, axis=(0, 2)), "heads")
    inv_rms = lax.rsqrt(totals / width + EPS)
    normed = (attended * inv_rms[None, :, None] * norm_gain[:, None, :]).astype(jnp.bfloat16)
    scaled = norm_gain[:, None, :] * grad_normed.astype(jnp.float32)
    inner_sum = lax.psum(jnp.sum(scaled * attended, axis=(0, 2)), "heads")
    grad_out = (
        inv_rms[None, :, None] * scaled - attended * (inv_rms**3 * inner_sum / width)[None, :, None]
    ).astype(jnp.bfloat16)
    grad_wide = grad_out.astype(jnp.float32)
    grad_mix = jnp.einsum("hte,hse->hts", grad_out, value_rows, preferred_element_type=jnp.float32)
    product = grad_mix * scores
    near_grads = [
        level_scale(number, head_dim)
        * jnp.sum(jnp.where((bucket == number) & causal, product, jnp.float32(0.0)), axis=2)
        for number in range(local_levels)
    ]
    far_grads = [
        level_scale(local_levels + depth, head_dim) * jnp.sum(grad_wide * far_terms[depth], axis=2)
        for depth in range(far_levels)
    ]
    grad_scores = (weights * grad_mix).astype(jnp.bfloat16)
    grad_q = jnp.einsum("hts,hsd->htd", grad_scores, key_rows, preferred_element_type=jnp.float32)
    grad_q = grad_q + jnp.sum(
        far_scale[..., None] * jnp.einsum("hte,mhde->mhtd", grad_wide, states, precision=HIGH), 0
    )
    scaled_queries = (far_scale[..., None] * queries[None]).astype(jnp.bfloat16)
    grad_states = jnp.einsum(
        "mhtd,hte->mhde", scaled_queries, grad_out, preferred_element_type=jnp.float32
    )
    grad_kv = jnp.zeros((heads_here, head_dim, head_dim), jnp.float32)
    for depth in range(far_levels):
        level_total = grad_states[depth]
        for step_bit in range(depth + 1):
            partner = pair_level(level_total, step_bit)
            if step_bit < depth:
                level_total = level_total + partner
            else:
                bit_set = block_index >> step_bit & 1
                grad_kv = grad_kv + jnp.where(bit_set == 0, partner, jnp.float32(0.0))
    grad_kv = grad_kv.astype(jnp.bfloat16)
    grad_k = jnp.einsum("hts,htd->hsd", grad_scores, queries, preferred_element_type=jnp.float32)
    grad_k = grad_k + jnp.einsum(
        "hse,hde->hsd", value_rows, grad_kv, preferred_element_type=jnp.float32
    )
    grad_v = jnp.einsum("hts,hte->hse", weighted, grad_out, preferred_element_type=jnp.float32)
    grad_v = grad_v + jnp.einsum(
        "hsd,hde->hse", key_rows, grad_kv, preferred_element_type=jnp.float32
    )
    grad_rates = jnp.stack(near_grads + far_grads, axis=1)
    return (
        normed,
        grad_q.astype(jnp.bfloat16),
        grad_k.astype(jnp.bfloat16),
        grad_v.astype(jnp.bfloat16),
        grad_rates,
    )


def solution(mesh):
    in_specs = (
        P("heads", "ctx", None),
        P("heads", "ctx", None),
        P("heads", "ctx", None),
        P("heads", None, "ctx"),
        P("heads", None),
        P("heads", "ctx", None),
    )
    out_specs = (
        P("heads", "ctx", None),
        P("heads", "ctx", None),
        P("heads", "ctx", None),
        P("heads", "ctx", None),
        P("heads", None, "ctx"),
    )
    return jax.shard_map(shards, mesh=mesh, in_specs=in_specs, out_specs=out_specs, check_vma=False)
```

profile of v0, /device:TPU:0, one launch (start us, length us, event | category | flops | bytes accessed | tf_op | source)
XLA Modules:
  0.0 86.8 jit_solution(17006751572486609093)
XLA Ops:
  0.6 0.0 copy-start
  0.7 0.9 %copy-done = bf16[4,256,128]{2,1,0:T(8,128)(2,1)S(1)} copy-done((bf16[4,256,128]{2,1,0:T(8,128)(2,1)S(1)}, bf16[4,256,128]{2,1,0:T(8,128)(2,1)}, u32[]{:S(2)}) %copy-start) | copy-done | bytes 262168
  1.6 1.2 %fusion.39 = f32[4,128,128]{2,1,0:T(8,128)S(1)} fusion(bf16[4,256,128]{2,1,0:T(8,128)(2,1)} %param.7, bf16[4,256,128]{2,1,0:T(8,128)(2,1)S(1)} %copy-done), kind=kOutput, calls=%fused_computation.115 | convolution fusion | flops 33554432 | bytes 786432 | tf_op jit(solution)/shard_map/hsd,hse->hde/dot_general | solution.py:52
  2.8 0.6 collective-permute-start
  3.4 0.2 fusion.20
  3.5 0.2 fusion.22
  3.7 0.8 collective-permute-done
  4.6 0.0 copy-start.9
  4.6 0.0 copy-start.1
  4.6 2.9 %collective-permute-start.1 = (f32[4,128,128]{2,1,0:T(8,128)S(1)}, f32[4,128,128]{2,1,0:T(8,128)S(1)}, u32[]{:S(2)}, u32[]{:S(2)}) collective-permute-start(f32[4,128,128]{2,1,0:T(8,128)S(1)} %get-tuple-element.42), channel_id=1, source_target_pairs={{0,2},{1,3},{2,0},{3,1},{4,6},{5,7},{6,4},{7,5},{8,10},{9,11},{10,... | collective-permute-start | bytes 786440 | tf_op jit(solution)/shard_map/ppermute | solution.py:15
  7.5 0.1 fusion.28
  7.7 0.0 copy-start.34
  7.8 6.3 %collective-permute-done.1 = f32[4,128,128]{2,1,0:T(8,128)S(1)} collective-permute-done((f32[4,128,128]{2,1,0:T(8,128)S(1)}, f32[4,128,128]{2,1,0:T(8,128)S(1)}, u32[]{:S(2)}, u32[]{:S(2)}) %collective-permute-start.1) | collective-permute-done | bytes 262176 | tf_op jit(solution)/shard_map/ppermute | solution.py:15
  14.1 0.7 select_bitcast_fusion.2
  14.9 1.8 %collective-permute-start.2 = (f32[4,128,128]{2,1,0:T(8,128)S(1)}, f32[4,128,128]{2,1,0:T(8,128)S(1)}, u32[]{:S(2)}, u32[]{:S(2)}) collective-permute-start(f32[4,128,128]{2,1,0:T(8,128)S(1)} %get-tuple-element.44), channel_id=1, source_target_pairs={{0,4},{1,5},{2,6},{3,7},{4,0},{5,1},{6,2},{7,3},{8,12},{9,13},{10,... | collective-permute-start | bytes 786440 | tf_op jit(solution)/shard_map/ppermute | solution.py:15
  16.7 0.1 copy.35
  16.9 0.9 %copy.42 = f32[4,256,128]{1,2,0:T(8,128)} copy(bf16[4,256,128]{2,1,0:T(8,128)(2,1)S(1)} %copy-done.2) | data formatting | bytes 786432 | tf_op jit(solution)/shard_map/convert_element_type | solution.py:103
  17.8 0.2 fusion.24
  18.0 0.2 fusion.26
  18.2 4.5 %collective-permute-done.2 = f32[4,128,128]{2,1,0:T(8,128)S(1)} collective-permute-done((f32[4,128,128]{2,1,0:T(8,128)S(1)}, f32[4,128,128]{2,1,0:T(8,128)S(1)}, u32[]{:S(2)}, u32[]{:S(2)}) %collective-permute-start.2) | collective-permute-done | bytes 262176 | tf_op jit(solution)/shard_map/ppermute | solution.py:15
  22.7 0.0 copy-start.13
  22.7 2.6 %collective-permute-start.3 = (f32[4,128,128]{2,1,0:T(8,128)S(1)}, f32[4,128,128]{2,1,0:T(8,128)S(1)}, u32[]{:S(2)}, u32[]{:S(2)}) collective-permute-start(f32[4,128,128]{2,1,0:T(8,128)S(1)} %get-tuple-element.46), channel_id=1, source_target_pairs={{0,8},{1,9},{2,10},{3,11},{4,12},{5,13},{6,14},{7,15},{8,0},{9,1},... | collective-permute-start | bytes 786440 | tf_op jit(solution)/shard_map/ppermute | solution.py:15
  25.3 2.0 %multiply_convert_fusion.3 = (bf16[4,256,256]{1,2,0:T(8,128)(2,1)S(1)}, f32[4,256,256]{1,2,0:T(8,128)}) fusion(f32[4,256]{1,0:T(4,128)S(1)} %get-tuple-element.50, pred[256,256]{0,1:T(8,128)(4,1)S(1)} %get-tuple-element.69, f32[4,256]{1,0:T(4,128)S(1)} %get-tuple-element.51, pred[256,256]{0,1:T(8,128)(4,1)S(1)} %get-tuple-element.70, ...), kind=kOutput, calls=%fused_computation.28 | convolution fusion | flops 72089600 | bytes 2723840 | tf_op jit(solution)/shard_map/htd,hsd->hts/dot_general | solution.py:65
  27.5 8.7 %collective-permute-done.3 = f32[4,128,128]{2,1,0:T(8,128)S(1)} collective-permute-done((f32[4,128,128]{2,1,0:T(8,128)S(1)}, f32[4,128,128]{2,1,0:T(8,128)S(1)}, u32[]{:S(2)}, u32[]{:S(2)}) %collective-permute-start.3) | collective-permute-done | bytes 262176 | tf_op jit(solution)/shard_map/ppermute | solution.py:15
  36.2 0.0 copy-start.7
  36.2 0.0 copy-start.32
  36.3 1.1 %multiply_reduce_fusion = (f32[4,256,128]{1,2,0:T(8,128)S(1)}, f32[4,4,256,128]{2,3,1,0:T(8,128)S(1)}) fusion(f32[4,4,256]{2,1,0:T(4,128)S(1)} %pad_maximum_fusion.3, bf16[4,256,128]{2,1,0:T(8,128)(2,1)S(1)} %copy-done.2, f32[1,4,128,128]{3,2,1,0:T(8,128)S(1)} %select_bitcast_fusion, f32[1,4,128,128]{3,2,1,0:T(8,128)S(1)} %get-tuple-element.45, ...), kind=kOutput, calls=%fused_computation.3 | convolution fusion | flops 807010304 | bytes 3948544 | tf_op jit(solution)/shard_map/htd,mhde->mhte/dot_general | solution.py:76
  37.4 1.1 %multiply_reduce_fusion.1 = (f32[256]{0:T(256)S(1)}, f32[256]{0:T(256)S(1)}, f32[4,256,128]{1,2,0:T(8,128)}) fusion(bf16[4,256,128]{1,2,0:T(8,128)(2,1)S(1)} %copy.35, f32[4,128]{1,0:T(4,128)S(1)} %copy-done.32, f32[4,256,128]{1,2,0:T(8,128)S(1)} %get-tuple-element.62, bf16[4,256,256]{1,2,0:T(8,128)(2,1)S(1)} %get-tuple-element.64, ...), kind=kOutput, calls=%fused_computation.43 | convolution fusion | flops 68025856 | bytes 2101248 | tf_op jit(solution)/shard_map/hts,hse->hte/dot_general | solution.py:67
  38.6 4.9 %all-reduce = (f32[256]{0:T(256)S(1)}, f32[256]{0:T(256)S(1)}) all-reduce(f32[256]{0:T(256)S(1)} %get-tuple-element.29, f32[256]{0:T(256)S(1)} %get-tuple-element.28), channel_id=1, replica_groups=mesh['heads'=2,'ctx'=16] {'heads'}, use_global_device_ids=true, to_apply=%region_2.3 | all-reduce | flops 512 | bytes 4096 | tf_op jit(solution)/shard_map/psum | solution.py:78
  43.5 1.4 %fusion.11 = (f32[4,256]{1,0:T(4,128)S(1)}, f32[4,256]{1,0:T(4,128)S(1)}, f32[4,256]{1,0:T(4,128)S(1)}, f32[4,256]{1,0:T(4,128)S(1)}, bf16[4,256,128]{1,2,0:T(8,128)(2,1)S(1)}, /*index=5*/bf16[4,256,128]{1,2,0:T(8,128)(2,1)S(1)}) fusion(f32[4,4,256,128]{2,3,1,0:T(8,128)S(1)} %get-tuple-element.63, f32[4,256,128]{1,2,0:T(8,128)} %get-tuple-element.66, ...), kind=kLoop, calls=%fused_computation.37 | loop fusion | flops 2355200 | bytes 3428352 | tf_op jit(solution)/shard_map/reduce_sum | solution.py:95
  45.0 2.3 %multiply_convert_fusion.2 = (bf16[4,256,256]{1,2,0:T(8,128)(2,1)S(1)}, f32[4,256,256]{1,2,0:T(8,128)S(1)}) fusion(f32[4,256]{1,0:T(4,128)} %copy-done.34, pred[256,256]{0,1:T(8,128)(4,1)S(1)} %get-tuple-element.69, f32[4,256]{1,0:T(4,128)} %copy-done.35, pred[256,256]{0,1:T(8,128)(4,1)S(1)} %get-tuple-element.70, f32[4,256]{1,0:T(4,128)} %copy-done.36, ...), kind=kOutput, calls=%fused_computation.26 | convolution fusion | flops 72089600 | bytes 2723840 | tf_op jit(solution)/shard_map/hte,hse->hts/dot_general | solution.py:87
  47.4 0.9 %select_reduce_fusion = (f32[4,256]{1,0:T(4,128)S(1)}, f32[4,256]{1,0:T(4,128)S(1)}, f32[4,256]{1,0:T(4,128)S(1)}, f32[4,256]{1,0:T(4,128)S(1)}, f32[4,256]{1,0:...) fusion(pred[256,256]{0,1:T(8,128)(4,1)S(1)} %get-tuple-element.69, ...), kind=kLoop, calls=%fused_computation.16 | loop fusion | flops 4971520 | bytes 2723840 | tf_op jit(solution)/shard_map/reduce_sum | solution.py:91
  48.3 0.0 copy-done.3
  48.3 0.4 convolution_bitcast_fusion.1
  48.8 0.8 slice_bitcast_fusion.7
  49.6 0.5 collective-permute-start.5
  50.1 0.5 collective-permute-start.4
  50.7 0.0 copy-start.8
  50.7 0.0 copy-start.12
  50.7 0.0 copy-start.14
  50.7 0.4 collective-permute-done.10
  51.1 0.4 collective-permute-done.5
  51.5 0.4 collective-permute-done.7
  51.8 0.8 fusion.36
  52.6 1.2 %collective-permute-start.11 = (f32[4,128,128]{2,1,0:T(8,128)S(1)}, f32[4,128,128]{2,1,0:T(8,128)S(1)}, u32[]{:S(2)}, u32[]{:S(2)}) collective-permute-start(f32[4,128,128]{2,1,0:T(8,128)S(1)} %get-tuple-element.38), channel_id=1, source_target_pairs={{0,2},{1,3},{2,0},{3,1},{4,6},{5,7},{6,4},{7,5},{8,10},{9,11},{10,... | collective-permute-start | bytes 786440 | tf_op jit(solution)/shard_map/ppermute | solution.py:15
  53.8 0.3 fusion.41
  54.1 0.9 %collective-permute-start.8 = (f32[4,128,128]{2,1,0:T(8,128)S(1)}, f32[4,128,128]{2,1,0:T(8,128)}, u32[]{:S(2)}, u32[]{:S(2)}) collective-permute-start(f32[4,128,128]{2,1,0:T(8,128)S(1)} %get-tuple-element.39), channel_id=1, source_target_pairs={{0,2},{1,3},{2,0},{3,1},{4,6},{5,7},{6,4},{7,5},{8,10},{9,11},{10,... | collective-permute-start | bytes 786440 | tf_op jit(solution)/shard_map/ppermute | solution.py:15
  55.0 6.8 %collective-permute-done.11 = f32[4,128,128]{2,1,0:T(8,128)S(1)} collective-permute-done((f32[4,128,128]{2,1,0:T(8,128)S(1)}, f32[4,128,128]{2,1,0:T(8,128)S(1)}, u32[]{:S(2)}, u32[]{:S(2)}) %collective-permute-start.11) | collective-permute-done | bytes 262176 | tf_op jit(solution)/shard_map/ppermute | solution.py:15
  61.8 0.4 collective-permute-start.12
  62.3 1.8 %fusion = f32[4,256,128]{1,2,0:T(8,128)} fusion(f32[4,4,256]{2,1,0:T(4,128)S(1)} %pad_maximum_fusion.3, f32[1,4,128,128]{3,2,1,0:T(8,128)S(1)} %copy-done.8, f32[1,4,128,128]{3,2,1,0:T(8,128)S(1)} %copy-done.14, f32[1,4,128,128]{3,2,1,0:T(8,128)S(1)} %copy-done.12, f32[1,4,128,128]{3,2,1,0:T(8,128)S(1)} %copy-done.10, ...), kind=kOutput, calls=%fused_computation.1 | convolution fusion | flops 807010304 | bytes 1851392 | tf_op jit(solution)/shard_map/hte,mhde->mhtd/dot_general | solution.py:101
  64.1 1.3 %copy.41 = f32[4,256,128]{2,1,0:T(8,128)S(1)} copy(f32[4,256,128]{1,2,0:T(8,128)} %fusion) | data formatting | bytes 1048576 | tf_op jit(solution)/shard_map/reduce_sum | solution.py:100
  65.4 0.8 copy.49
  66.3 0.3 fusion.40
  66.6 1.6 %collective-permute-start.6 = (f32[4,128,128]{2,1,0:T(8,128)S(1)}, f32[4,128,128]{2,1,0:T(8,128)S(1)}, u32[]{:S(2)}, u32[]{:S(2)}) collective-permute-start(f32[4,128,128]{2,1,0:T(8,128)S(1)} %copy-done.15), channel_id=1, source_target_pairs={{0,2},{1,3},{2,0},{3,1},{4,6},{5,7},{6,4},{7,5},{8,10},{9,11},{10,... | collective-permute-start | bytes 786440 | tf_op jit(solution)/shard_map/ppermute | solution.py:15
  68.1 1.0 %add.366 = f32[4,128,128]{2,1,0:T(8,128)S(1)} add(f32[4,128,128]{2,1,0:T(8,128)S(1)} %get-tuple-element.39, f32[4,128,128]{2,1,0:T(8,128)} %collective-permute-done.8) | non-fusion elementwise | flops 65536 | bytes 786432 | tf_op jit(solution)/shard_map/add | solution.py:113
  69.1 1.4 %collective-permute-start.9 = (f32[4,128,128]{2,1,0:T(8,128)S(1)}, f32[4,128,128]{2,1,0:T(8,128)S(1)}, u32[]{:S(2)}, u32[]{:S(2)}) collective-permute-start(f32[4,128,128]{2,1,0:T(8,128)S(1)} %add.366), channel_id=1, source_target_pairs={{0,4},{1,5},{2,6},{3,7},{4,0},{5,1},{6,2},{7,3},{8,12},{9,13},{10,... | collective-permute-start | bytes 786440 | tf_op jit(solution)/shard_map/ppermute | solution.py:15
  70.5 1.0 %add.370 = f32[4,128,128]{2,1,0:T(8,128)S(1)} add(f32[4,128,128]{2,1,0:T(8,128)S(1)} %add.369, f32[4,128,128]{2,1,0:T(8,128)} %collective-permute-done.12) | non-fusion elementwise | flops 65536 | bytes 786432 | tf_op jit(solution)/shard_map/add | solution.py:113
  71.5 2.1 %collective-permute-start.13 = (f32[4,128,128]{2,1,0:T(8,128)S(1)}, f32[4,128,128]{2,1,0:T(8,128)S(1)}, u32[]{:S(2)}, u32[]{:S(2)}) collective-permute-start(f32[4,128,128]{2,1,0:T(8,128)S(1)} %add.370), channel_id=1, source_target_pairs={{0,8},{1,9},{2,10},{3,11},{4,12},{5,13},{6,14},{7,15},{8,0},{9,1},... | collective-permute-start | bytes 786440 | tf_op jit(solution)/shard_map/ppermute | solution.py:15
  73.6 1.0 %fusion.3 = bf16[4,256,128]{2,1,0:T(8,128)(2,1)} fusion(f32[4,256,128]{2,1,0:T(8,128)S(1)} %copy.41, bf16[4,256,256]{1,2,0:T(8,128)(2,1)S(1)} %get-tuple-element.67, bf16[4,256,128]{2,1,0:T(8,128)(2,1)S(1)} %copy-done.1), kind=kOutput, calls=%fused_computation.12 | convolution fusion | flops 67371008 | bytes 1572864 | tf_op jit(solution)/shard_map/hts,hsd->htd/dot_general | solution.py:99
  74.7 5.8 %collective-permute-done.9 = f32[4,128,128]{2,1,0:T(8,128)S(1)} collective-permute-done((f32[4,128,128]{2,1,0:T(8,128)S(1)}, f32[4,128,128]{2,1,0:T(8,128)S(1)}, u32[]{:S(2)}, u32[]{:S(2)}) %collective-permute-start.9) | collective-permute-done | bytes 262176 | tf_op jit(solution)/shard_map/ppermute | solution.py:15
  80.5 3.4 %collective-permute-done.13 = f32[4,128,128]{2,1,0:T(8,128)S(1)} collective-permute-done((f32[4,128,128]{2,1,0:T(8,128)S(1)}, f32[4,128,128]{2,1,0:T(8,128)S(1)}, u32[]{:S(2)}, u32[]{:S(2)}) %collective-permute-start.13) | collective-permute-done | bytes 262176 | tf_op jit(solution)/shard_map/ppermute | solution.py:15
  84.0 1.0 %add_convert_fusion = bf16[4,128,128]{2,1,0:T(8,128)(2,1)S(1)} fusion(f32[4,128,128]{2,1,0:T(8,128)S(1)} %collective-permute-done.13, f32[4,128,128]{2,1,0:T(8,128)S(1)} %collective-permute-done.9, f32[4,128,128]{2,1,0:T(8,128)S(1)} %collective-permute-done.6, f32[4,128,128]{2,1,0:T(8,128)} %collective-permute-done.4, pred[]{:T(512)S(6)} %eq.94, ...), kind=kLoop, calls=%fused_computation.73 | loop fusion | flops 524288 | bytes 1179652 | tf_op jit(solution)/shard_map/convert_element_type | solution.py:117
  85.0 0.9 %fusion.4 = bf16[4,256,128]{2,1,0:T(8,128)(2,1)} fusion(f32[4,256,128]{2,1,0:T(8,128)S(1)} %fusion.41, bf16[4,256,128]{2,1,0:T(8,128)(2,1)S(1)} %copy-done.1, bf16[4,128,128]{2,1,0:T(8,128)(2,1)S(1)} %add_convert_fusion), kind=kOutput, calls=%fused_computation.13 | convolution fusion | flops 33816576 | bytes 1179648 | tf_op jit(solution)/shard_map/hsd,hde->hse/dot_general | solution.py:123
  85.9 0.9 %fusion.5 = bf16[4,256,128]{2,1,0:T(8,128)(2,1)} fusion(f32[4,256,128]{2,1,0:T(8,128)S(1)} %fusion.40, bf16[4,128,128]{2,1,0:T(8,128)(2,1)S(1)} %add_convert_fusion, bf16[4,256,128]{2,1,0:T(8,128)(2,1)S(1)} %copy-done), kind=kOutput, calls=%fused_computation.14 | convolution fusion | flops 33816576 | bytes 1179648 | tf_op jit(solution)/shard_map/hse,hde->hsd/dot_general | solution.py:119
  (100 shorter events, 0.5 us)
Async XLA Ops:
  0.6 1.0 %copy-start = (bf16[4,256,128]{2,1,0:T(8,128)(2,1)S(1)}, bf16[4,256,128]{2,1,0:T(8,128)(2,1)}, u32[]{:S(2)}) copy-start(bf16[4,256,128]{2,1,0:T(8,128)(2,1)} %param.8) | copy-start | bytes 786436
  0.6 7.0 %copy-start.31 = (f32[4,13,256]{2,0,1:T(4,128)S(1)}, f32[4,13,256]{2,0,1:T(4,128)}, u32[]{:S(2)}) copy-start(f32[4,13,256]{2,0,1:T(4,128)} %param.9) | copy-start | bytes 159748
  0.7 16.0 %copy-start.30 = (bf16[4,256,128]{2,1,0:T(8,128)(2,1)S(1)}, bf16[4,256,128]{2,1,0:T(8,128)(2,1)}, u32[]{:S(2)}) copy-start(bf16[4,256,128]{2,1,0:T(8,128)(2,1)} %param.11) | copy-start | bytes 786436
  0.7 16.2 %copy-start.2 = (bf16[4,256,128]{2,1,0:T(8,128)(2,1)S(1)}, bf16[4,256,128]{2,1,0:T(8,128)(2,1)}, u32[]{:S(2)}) copy-start(bf16[4,256,128]{2,1,0:T(8,128)(2,1)} %param.6) | copy-start | bytes 786436
  2.8 1.7 %collective-permute-start = (f32[4,128,128]{2,1,0:T(8,128)S(1)}, f32[4,128,128]{2,1,0:T(8,128)S(1)}, u32[]{:S(2)}, u32[]{:S(2)}) collective-permute-start(f32[4,128,128]{2,1,0:T(8,128)S(1)} %fusion.39), channel_id=1, source_target_pairs={{0,1},{1,0},{2,3},{3,2},{4,5},{5,4},{6,7},{7,6},{8,9},{9,8},{10,11... | collective-permute-start | bytes 786440 | tf_op jit(solution)/shard_map/ppermute | solution.py:15
  3.7 23.6 %copy-start.16 = (pred[256,256]{0,1:T(8,128)(4,1)}, pred[256,256]{0,1:T(8,128)(4,1)S(1)}, u32[]{:S(2)}) copy-start(pred[256,256]{0,1:T(8,128)(4,1)S(1)} %get-tuple-element.71) | copy-start | bytes 196612
  3.7 23.6 %copy-start.18 = (pred[256,256]{0,1:T(8,128)(4,1)}, pred[256,256]{0,1:T(8,128)(4,1)S(1)}, u32[]{:S(2)}) copy-start(pred[256,256]{0,1:T(8,128)(4,1)S(1)} %get-tuple-element.72) | copy-start | bytes 196612
  4.6 31.7 %copy-start.9 = (f32[1,4,128,128]{3,2,1,0:T(8,128)}, f32[1,4,128,128]{3,2,1,0:T(8,128)S(1)}, u32[]{:S(2)}) copy-start(f32[1,4,128,128]{3,2,1,0:T(8,128)S(1)} %get-tuple-element.41) | copy-start | bytes 786436
  4.6 20.7 %copy-start.1 = (bf16[4,256,128]{2,1,0:T(8,128)(2,1)S(1)}, bf16[4,256,128]{2,1,0:T(8,128)(2,1)}, u32[]{:S(2)}) copy-start(bf16[4,256,128]{2,1,0:T(8,128)(2,1)} %param.7) | copy-start | bytes 786436
  4.6 9.5 %collective-permute-start.1 = (f32[4,128,128]{2,1,0:T(8,128)S(1)}, f32[4,128,128]{2,1,0:T(8,128)S(1)}, u32[]{:S(2)}, u32[]{:S(2)}) collective-permute-start(f32[4,128,128]{2,1,0:T(8,128)S(1)} %get-tuple-element.42), channel_id=1, source_target_pairs={{0,2},{1,3},{2,0},{3,1},{4,6},{5,7},{6,4},{7,5},{8,10},{9,11},{10,... | collective-permute-start | bytes 786440 | tf_op jit(solution)/shard_map/ppermute | solution.py:15
  7.6 19.7 %copy-start.20 = (pred[256,256]{0,1:T(8,128)(4,1)}, pred[256,256]{0,1:T(8,128)(4,1)S(1)}, u32[]{:S(2)}) copy-start(pred[256,256]{0,1:T(8,128)(4,1)S(1)} %fusion.28) | copy-start | bytes 196612
  7.7 19.7 %copy-start.33 = (f32[4,256]{1,0:T(4,128)}, f32[4,256]{1,0:T(4,128)S(1)}, u32[]{:S(2)}) copy-start(f32[4,256]{1,0:T(4,128)S(1)} %get-tuple-element.47) | copy-start | bytes 12292
  7.7 19.6 %copy-start.34 = (f32[4,256]{1,0:T(4,128)}, f32[4,256]{1,0:T(4,128)S(1)}, u32[]{:S(2)}) copy-start(f32[4,256]{1,0:T(4,128)S(1)} %get-tuple-element.50) | copy-start | bytes 12292
  7.7 19.6 %copy-start.35 = (f32[4,256]{1,0:T(4,128)}, f32[4,256]{1,0:T(4,128)S(1)}, u32[]{:S(2)}) copy-start(f32[4,256]{1,0:T(4,128)S(1)} %get-tuple-element.51) | copy-start | bytes 12292
  7.7 19.6 %copy-start.36 = (f32[4,256]{1,0:T(4,128)}, f32[4,256]{1,0:T(4,128)S(1)}, u32[]{:S(2)}) copy-start(f32[4,256]{1,0:T(4,128)S(1)} %get-tuple-element.52) | copy-start | bytes 12292
  7.7 19.6 %copy-start.37 = (f32[4,256]{1,0:T(4,128)}, f32[4,256]{1,0:T(4,128)S(1)}, u32[]{:S(2)}) copy-start(f32[4,256]{1,0:T(4,128)S(1)} %get-tuple-element.53) | copy-start | bytes 12292
  7.7 19.6 %copy-start.38 = (f32[4,256]{1,0:T(4,128)}, f32[4,256]{1,0:T(4,128)S(1)}, u32[]{:S(2)}) copy-start(f32[4,256]{1,0:T(4,128)S(1)} %get-tuple-element.54) | copy-start | bytes 12292
  7.8 19.6 %copy-start.39 = (f32[4,256]{1,0:T(4,128)}, f32[4,256]{1,0:T(4,128)S(1)}, u32[]{:S(2)}) copy-start(f32[4,256]{1,0:T(4,128)S(1)} %get-tuple-element.55) | copy-start | bytes 12292
  7.8 19.6 %copy-start.40 = (f32[4,256]{1,0:T(4,128)}, f32[4,256]{1,0:T(4,128)S(1)}, u32[]{:S(2)}) copy-start(f32[4,256]{1,0:T(4,128)S(1)} %get-tuple-element.56) | copy-start | bytes 12292
  7.8 19.6 %copy-start.41 = (f32[4,256]{1,0:T(4,128)}, f32[4,256]{1,0:T(4,128)S(1)}, u32[]{:S(2)}) copy-start(f32[4,256]{1,0:T(4,128)S(1)} %get-tuple-element.57) | copy-start | bytes 12292
  14.9 7.8 %collective-permute-start.2 = (f32[4,128,128]{2,1,0:T(8,128)S(1)}, f32[4,128,128]{2,1,0:T(8,128)S(1)}, u32[]{:S(2)}, u32[]{:S(2)}) collective-permute-start(f32[4,128,128]{2,1,0:T(8,128)S(1)} %get-tuple-element.44), channel_id=1, source_target_pairs={{0,4},{1,5},{2,6},{3,7},{4,0},{5,1},{6,2},{7,3},{8,12},{9,13},{10,... | collective-permute-start | bytes 786440 | tf_op jit(solution)/shard_map/ppermute | solution.py:15
  18.0 9.5 %copy-start.22 = (pred[256,256]{0,1:T(8,128)(4,1)}, pred[256,256]{0,1:T(8,128)(4,1)S(1)}, u32[]{:S(2)}) copy-start(pred[256,256]{0,1:T(8,128)(4,1)S(1)} %get-tuple-element.73) | copy-start | bytes 196612
  18.0 9.5 %copy-start.24 = (pred[256,256]{0,1:T(8,128)(4,1)}, pred[256,256]{0,1:T(8,128)(4,1)S(1)}, u32[]{:S(2)}) copy-start(pred[256,256]{0,1:T(8,128)(4,1)S(1)} %get-tuple-element.74) | copy-start | bytes 196612
  18.1 9.3 %copy-start.26 = (pred[256,256]{0,1:T(8,128)(4,1)}, pred[256,256]{0,1:T(8,128)(4,1)S(1)}, u32[]{:S(2)}) copy-start(pred[256,256]{0,1:T(8,128)(4,1)S(1)} %get-tuple-element.75) | copy-start | bytes 196612
  18.2 9.3 %copy-start.28 = (pred[256,256]{0,1:T(8,128)(4,1)}, pred[256,256]{0,1:T(8,128)(4,1)S(1)}, u32[]{:S(2)}) copy-start(pred[256,256]{0,1:T(8,128)(4,1)S(1)} %get-tuple-element.76) | copy-start | bytes 196612
  22.7 13.6 %copy-start.13 = (f32[1,4,128,128]{3,2,1,0:T(8,128)}, f32[1,4,128,128]{3,2,1,0:T(8,128)S(1)}, u32[]{:S(2)}) copy-start(f32[1,4,128,128]{3,2,1,0:T(8,128)S(1)} %get-tuple-element.45) | copy-start | bytes 786436
  22.7 13.5 %collective-permute-start.3 = (f32[4,128,128]{2,1,0:T(8,128)S(1)}, f32[4,128,128]{2,1,0:T(8,128)S(1)}, u32[]{:S(2)}, u32[]{:S(2)}) collective-permute-start(f32[4,128,128]{2,1,0:T(8,128)S(1)} %get-tuple-element.46), channel_id=1, source_target_pairs={{0,8},{1,9},{2,10},{3,11},{4,12},{5,13},{6,14},{7,15},{8,0},{9,1},... | collective-permute-start | bytes 786440 | tf_op jit(solution)/shard_map/ppermute | solution.py:15
  25.3 10.9 %copy-start.11 = (f32[1,4,128,128]{3,2,1,0:T(8,128)S(1)}, f32[1,4,128,128]{3,2,1,0:T(8,128)}, u32[]{:S(2)}) copy-start(f32[1,4,128,128]{3,2,1,0:T(8,128)} %get-tuple-element.43) | copy-start | bytes 786436
  27.5 9.9 %copy-start.4 = (bf16[4,256,256]{1,2,0:T(8,128)(2,1)}, bf16[4,256,256]{1,2,0:T(8,128)(2,1)S(1)}, u32[]{:S(2)}) copy-start(bf16[4,256,256]{1,2,0:T(8,128)(2,1)S(1)} %get-tuple-element.64) | copy-start | bytes 1572868
  36.2 2.3 %copy-start.7 = (f32[1,4,128,128]{3,2,1,0:T(8,128)}, f32[1,4,128,128]{3,2,1,0:T(8,128)S(1)}, u32[]{:S(2)}) copy-start(f32[1,4,128,128]{3,2,1,0:T(8,128)S(1)} %select_bitcast_fusion) | copy-start | bytes 786436
  36.2 1.2 %copy-start.32 = (f32[4,128]{1,0:T(4,128)S(1)}, f32[4,128]{1,0:T(4,128)}, u32[]{:S(2)}) copy-start(f32[4,128]{1,0:T(4,128)} %param.10) | copy-start | bytes 6148
  44.9 2.4 %copy-start.6 = (f32[4,256,256]{1,2,0:T(8,128)S(1)}, f32[4,256,256]{1,2,0:T(8,128)}, u32[]{:S(2)}) copy-start(f32[4,256,256]{1,2,0:T(8,128)} %get-tuple-element.65) | copy-start | bytes 3145732
  44.9 2.4 %copy-start.17 = (pred[256,256]{0,1:T(8,128)(4,1)S(1)}, pred[256,256]{0,1:T(8,128)(4,1)}, u32[]{:S(2)}) copy-start(pred[256,256]{0,1:T(8,128)(4,1)} %copy-done.16) | copy-start | bytes 196612
  44.9 2.4 %copy-start.19 = (pred[256,256]{0,1:T(8,128)(4,1)S(1)}, pred[256,256]{0,1:T(8,128)(4,1)}, u32[]{:S(2)}) copy-start(pred[256,256]{0,1:T(8,128)(4,1)} %copy-done.18) | copy-start | bytes 196612
  44.9 2.4 %copy-start.21 = (pred[256,256]{0,1:T(8,128)(4,1)S(1)}, pred[256,256]{0,1:T(8,128)(4,1)}, u32[]{:S(2)}) copy-start(pred[256,256]{0,1:T(8,128)(4,1)} %copy-done.20) | copy-start | bytes 196612
  44.9 2.4 %copy-start.23 = (pred[256,256]{0,1:T(8,128)(4,1)S(1)}, pred[256,256]{0,1:T(8,128)(4,1)}, u32[]{:S(2)}) copy-start(pred[256,256]{0,1:T(8,128)(4,1)} %copy-done.22) | copy-start | bytes 196612
  45.0 2.4 %copy-start.25 = (pred[256,256]{0,1:T(8,128)(4,1)S(1)}, pred[256,256]{0,1:T(8,128)(4,1)}, u32[]{:S(2)}) copy-start(pred[256,256]{0,1:T(8,128)(4,1)} %copy-done.24) | copy-start | bytes 196612
  45.0 2.4 %copy-start.27 = (pred[256,256]{0,1:T(8,128)(4,1)S(1)}, pred[256,256]{0,1:T(8,128)(4,1)}, u32[]{:S(2)}) copy-start(pred[256,256]{0,1:T(8,128)(4,1)} %copy-done.26) | copy-start | bytes 196612
  45.0 2.4 %copy-start.29 = (pred[256,256]{0,1:T(8,128)(4,1)S(1)}, pred[256,256]{0,1:T(8,128)(4,1)}, u32[]{:S(2)}) copy-start(pred[256,256]{0,1:T(8,128)(4,1)} %copy-done.28) | copy-start | bytes 196612
  47.3 1.0 %copy-start.3 = (f32[4,256,128]{1,2,0:T(8,128)S(1)}, f32[4,256,128]{1,2,0:T(8,128)}, u32[]{:S(2)}) copy-start(f32[4,256,128]{1,2,0:T(8,128)} %copy.42) | copy-start | bytes 1572868
  48.8 5.1 %copy-start.5 = (bf16[4,256,256]{1,2,0:T(8,128)(2,1)S(1)}, bf16[4,256,256]{1,2,0:T(8,128)(2,1)}, u32[]{:S(2)}) copy-start(bf16[4,256,256]{1,2,0:T(8,128)(2,1)} %copy-done.4) | copy-start | bytes 1572868
  49.5 1.5 %collective-permute-start.10 = (f32[4,128,128]{2,1,0:T(8,128)S(1)}, f32[4,128,128]{2,1,0:T(8,128)S(1)}, u32[]{:S(2)}, u32[]{:S(2)}) collective-permute-start(f32[4,128,128]{2,1,0:T(8,128)S(1)} %get-tuple-element.34), channel_id=1, source_target_pairs={{0,1},{1,0},{2,3},{3,2},{4,5},{5,4},{6,7},{7,6},{8,9},{9,8},{10,11... | collective-permute-start | bytes 786440 | tf_op jit(solution)/shard_map/ppermute | solution.py:15
  49.6 1.9 %collective-permute-start.5 = (f32[4,128,128]{2,1,0:T(8,128)S(1)}, f32[4,128,128]{2,1,0:T(8,128)S(1)}, u32[]{:S(2)}, u32[]{:S(2)}) collective-permute-start(f32[4,128,128]{2,1,0:T(8,128)S(1)} %get-tuple-element.36), channel_id=1, source_target_pairs={{0,1},{1,0},{2,3},{3,2},{4,5},{5,4},{6,7},{7,6},{8,9},{9,8},{10,11... | collective-permute-start | bytes 786440 | tf_op jit(solution)/shard_map/ppermute | solution.py:15
  50.1 1.8 %collective-permute-start.7 = (f32[4,128,128]{2,1,0:T(8,128)S(1)}, f32[4,128,128]{2,1,0:T(8,128)S(1)}, u32[]{:S(2)}, u32[]{:S(2)}) collective-permute-start(f32[4,128,128]{2,1,0:T(8,128)S(1)} %get-tuple-element.35), channel_id=1, source_target_pairs={{0,1},{1,0},{2,3},{3,2},{4,5},{5,4},{6,7},{7,6},{8,9},{9,8},{10,11... | collective-permute-start | bytes 786440 | tf_op jit(solution)/shard_map/ppermute | solution.py:15
  50.1 24.6 %collective-permute-start.4 = (f32[4,128,128]{2,1,0:T(8,128)}, f32[4,128,128]{2,1,0:T(8,128)}, u32[]{:S(2)}, u32[]{:S(2)}) collective-permute-start(f32[4,128,128]{2,1,0:T(8,128)} %get-tuple-element.33), channel_id=1, source_target_pairs={{0,1},{1,0},{2,3},{3,2},{4,5},{5,4},{6,7},{7,6},{8,9},{9,8},{10,11... | collective-permute-start | bytes 786440 | tf_op jit(solution)/shard_map/ppermute | solution.py:15
  50.7 11.6 %copy-start.8 = (f32[1,4,128,128]{3,2,1,0:T(8,128)S(1)}, f32[1,4,128,128]{3,2,1,0:T(8,128)}, u32[]{:S(2)}) copy-start(f32[1,4,128,128]{3,2,1,0:T(8,128)} %copy-done.7) | copy-start | bytes 786436
  50.7 11.6 %copy-start.10 = (f32[1,4,128,128]{3,2,1,0:T(8,128)S(1)}, f32[1,4,128,128]{3,2,1,0:T(8,128)}, u32[]{:S(2)}) copy-start(f32[1,4,128,128]{3,2,1,0:T(8,128)} %copy-done.9) | copy-start | bytes 786436
  50.7 11.6 %copy-start.12 = (f32[1,4,128,128]{3,2,1,0:T(8,128)S(1)}, f32[1,4,128,128]{3,2,1,0:T(8,128)}, u32[]{:S(2)}) copy-start(f32[1,4,128,128]{3,2,1,0:T(8,128)} %get-tuple-element.43) | copy-start | bytes 786436
  50.7 11.6 %copy-start.14 = (f32[1,4,128,128]{3,2,1,0:T(8,128)S(1)}, f32[1,4,128,128]{3,2,1,0:T(8,128)}, u32[]{:S(2)}) copy-start(f32[1,4,128,128]{3,2,1,0:T(8,128)} %copy-done.13) | copy-start | bytes 786436
  52.6 9.2 %collective-permute-start.11 = (f32[4,128,128]{2,1,0:T(8,128)S(1)}, f32[4,128,128]{2,1,0:T(8,128)S(1)}, u32[]{:S(2)}, u32[]{:S(2)}) collective-permute-start(f32[4,128,128]{2,1,0:T(8,128)S(1)} %get-tuple-element.38), channel_id=1, source_target_pairs={{0,2},{1,3},{2,0},{3,1},{4,6},{5,7},{6,4},{7,5},{8,10},{9,11},{10,... | collective-permute-start | bytes 786440 | tf_op jit(solution)/shard_map/ppermute | solution.py:15
  53.8 10.3 %copy-start.42 = (f32[4,13,256]{2,0,1:T(4,128)}, f32[4,13,256]{2,0,1:T(4,128)S(1)}, u32[]{:S(2)}) copy-start(f32[4,13,256]{2,0,1:T(4,128)S(1)} %constant_dynamic-update-slice_fusion) | copy-start | bytes 159748
  54.1 14.0 %collective-permute-start.8 = (f32[4,128,128]{2,1,0:T(8,128)S(1)}, f32[4,128,128]{2,1,0:T(8,128)}, u32[]{:S(2)}, u32[]{:S(2)}) collective-permute-start(f32[4,128,128]{2,1,0:T(8,128)S(1)} %get-tuple-element.39), channel_id=1, source_target_pairs={{0,2},{1,3},{2,0},{3,1},{4,6},{5,7},{6,4},{7,5},{8,10},{9,11},{10,... | collective-permute-start | bytes 786440 | tf_op jit(solution)/shard_map/ppermute | solution.py:15
  61.8 8.7 %collective-permute-start.12 = (f32[4,128,128]{2,1,0:T(8,128)S(1)}, f32[4,128,128]{2,1,0:T(8,128)}, u32[]{:S(2)}, u32[]{:S(2)}) collective-permute-start(f32[4,128,128]{2,1,0:T(8,128)S(1)} %add.369), channel_id=1, source_target_pairs={{0,4},{1,5},{2,6},{3,7},{4,0},{5,1},{6,2},{7,3},{8,12},{9,13},{10,... | collective-permute-start | bytes 786440 | tf_op jit(solution)/shard_map/ppermute | solution.py:15
  64.1 2.4 %copy-start.15 = (f32[4,128,128]{2,1,0:T(8,128)S(1)}, f32[4,128,128]{2,1,0:T(8,128)}, u32[]{:S(2)}) copy-start(f32[4,128,128]{2,1,0:T(8,128)} %get-tuple-element.37) | copy-start | bytes 786436
  66.6 8.1 %collective-permute-start.6 = (f32[4,128,128]{2,1,0:T(8,128)S(1)}, f32[4,128,128]{2,1,0:T(8,128)S(1)}, u32[]{:S(2)}, u32[]{:S(2)}) collective-permute-start(f32[4,128,128]{2,1,0:T(8,128)S(1)} %copy-done.15), channel_id=1, source_target_pairs={{0,2},{1,3},{2,0},{3,1},{4,6},{5,7},{6,4},{7,5},{8,10},{9,11},{10,... | collective-permute-start | bytes 786440 | tf_op jit(solution)/shard_map/ppermute | solution.py:15
  69.1 11.4 %collective-permute-start.9 = (f32[4,128,128]{2,1,0:T(8,128)S(1)}, f32[4,128,128]{2,1,0:T(8,128)S(1)}, u32[]{:S(2)}, u32[]{:S(2)}) collective-permute-start(f32[4,128,128]{2,1,0:T(8,128)S(1)} %add.366), channel_id=1, source_target_pairs={{0,4},{1,5},{2,6},{3,7},{4,0},{5,1},{6,2},{7,3},{8,12},{9,13},{10,... | collective-permute-start | bytes 786440 | tf_op jit(solution)/shard_map/ppermute | solution.py:15
  71.5 12.4 %collective-permute-start.13 = (f32[4,128,128]{2,1,0:T(8,128)S(1)}, f32[4,128,128]{2,1,0:T(8,128)S(1)}, u32[]{:S(2)}, u32[]{:S(2)}) collective-permute-start(f32[4,128,128]{2,1,0:T(8,128)S(1)} %add.370), channel_id=1, source_target_pairs={{0,8},{1,9},{2,10},{3,11},{4,12},{5,13},{6,14},{7,15},{8,0},{9,1},... | collective-permute-start | bytes 786440 | tf_op jit(solution)/shard_map/ppermute | solution.py:15
where the time goes:
time: 87.2 us; the launch traced here: 86.8 us
  waiting for transfers between devices  37.5 us (43%)
  starting transfers between devices  16.6 us (19%)
  matrix products  13.5 us (15%)
  other arithmetic  7.87 us (9%)
  local copies, waits for them, and re-layouts  5.16 us (6%)
  blocking collectives  4.91 us (6%)
  between operations  1.32 us (2%)
    ppermute x14, waiting for transfers between devices, from_partner(): return lax.ppermute(value, axis, pairs)  37.5 us
    ppermute x14, starting transfers between devices, from_partner(): return lax.ppermute(value, axis, pairs)  16.6 us
    psum x1, blocking collectives, shards(): totals = lax.psum(jnp.sum(attended * attended, axis=(0, 2)), 'heads')  4.91 us
    add x4, other arithmetic, shards(): level_total = level_total + partner  2.78 us
    dot_general x1, matrix products, shards(): jnp.einsum('hte,hse->hts', grad_out, value_rows, preferred_element_type=j...  2.28 us
    unnamed x88, local copies, waits for them, and re-layouts  2.15 us
    dot_general x1, matrix products, shards(): jnp.einsum('htd,hsd->hts', queries, key_rows, preferred_element_type=jnp....  2.01 us
    dot_general x1, matrix products, shards(): jnp.einsum('hte,mhde->mhtd', grad_wide, states, precision=HIGH)  1.84 us
  transfers between devices with their start and end apart: 14, of which 10 were waited for; matrix products, arithmetic and copies ran while one was open for 14% of the time, Pallas kernels for 0%

commit v1 on v0

v1 whole, which is shorter than its diff:
```python
import functools
import math

import jax
import jax.numpy as jnp
from jax import lax
from jax.experimental import pallas as pl
from jax.experimental.pallas import tpu as pltpu
from jax.sharding import PartitionSpec as P

EPS = 1e-06
MESH = pl.DeviceIdType.MESH
F32 = jnp.float32
BF16 = jnp.bfloat16


def level_scale(number, head_dim):
    return 2.0 ** (-max(number - 1, 0) / 2.0) / math.sqrt(head_dim)


def dot(a, b):
    return jnp.dot(a, b, preferred_element_type=F32)


def dot_nt(a, b):
    return lax.dot_general(a, b, (((1,), (1,)), ((), ())), preferred_element_type=F32)


def kernel(
    n_ctx, n_heads, chunks,
    q_ref, k_ref, v_ref, lw_ref, gain_ref, gn_ref,
    normed_ref, gq_ref, gk_ref, gv_ref, glw_ref,
    bucket_ref, qt_ref, scores_ref, weights_ref, weighted_ref, sq_ref, att_ref, scaled_ref, gt_ref,
    states_ref, gk_acc, gv_acc,
    gsum, rcv, gs, rs, tx, brcv, abuf, hx, hx_in,
    fs_sem, fr_sem, gas_sem, gar_sem, rss_sem, rsr_sem, bs_sem, br_sem, hs_sem, hr_sem,
):
    heads, tokens, dim = q_ref.shape
    far = n_ctx.bit_length() - 1
    local = tokens.bit_length()
    width = heads * n_heads * dim
    rows = heads * dim
    part = rows // chunks
    per_chunk = heads // chunks
    me = lax.axis_index("ctx")
    mine = lax.axis_index("heads")
    bits = [(me // 2**i) % 2 for i in range(far)]

    def peer(j):
        other = me
        for i in range(far):
            if j >> i & 1:
                other = other + (1 - 2 * bits[i]) * 2**i
        return other

    def peer_bits(j):
        return [1 - bits[i] if j >> i & 1 else bits[i] for i in range(far)]

    def place(which, m, c):
        start = c * part
        for i in range(m):
            start = start + which[i] * (part >> (i + 1))
        return start

    def span(start, size):
        return pl.ds(pl.multiple_of(start, 8), size)

    barrier = pltpu.get_barrier_semaphore()
    friends = list(range(1, n_ctx // 2)) + [n_ctx // 2]
    for j in friends:
        pl.semaphore_signal(barrier, inc=1, device_id={"ctx": peer(j)}, device_id_type=MESH)
    for j in range(1, n_heads):
        pl.semaphore_signal(
            barrier, inc=1, device_id={"heads": (mine + j) % n_heads}, device_id_type=MESH
        )

    def key_value(h):
        gsum[0, h * dim : (h + 1) * dim, :] = dot(k_ref[h].T, v_ref[h])

    def remote(src, dst, ssem, rsem, target, axis="ctx"):
        return pltpu.make_async_remote_copy(
            src_ref=src, dst_ref=dst, send_sem=ssem, recv_sem=rsem,
            device_id={axis: target}, device_id_type=MESH,
        )

    def fwd_copy(m, c):
        where = span(place(bits, m, c), part >> m)
        return remote(
            gsum.at[m, where, :], rcv.at[m, where, :], fs_sem.at[m, c], fr_sem.at[m, c], peer(2**m)
        )

    def gather_copies(m, c):
        where = span(place(bits, m, c), part >> m)
        return [
            remote(rcv.at[m, where, :], rcv.at[m, where, :], gas_sem.at[m, c], gar_sem.at[m, c], peer(j))
            for j in range(1, 2**m)
        ]

    def fwd_step(m, c):
        fwd_copy(m, c).wait_recv()
        if m < far - 1:
            half = span(place(bits, m + 1, c), part >> (m + 1))
            gsum[m + 1, half, :] = gsum[m, half, :] + rcv[m, half, :]
            fwd_copy(m + 1, c).start()
        if m > 0:

            @pl.when(bits[m] == 1)
            def _():
                for copy in gather_copies(m, c):
                    copy.start()

    def gather_rows(m):
        return part - (part >> m)

    def local_wait(buffer, count, sem):
        pltpu.make_async_copy(buffer.at[pl.ds(0, count), :], buffer.at[pl.ds(0, count), :], sem).wait()

    s_pos = lax.broadcasted_iota(jnp.int32, (tokens, tokens), 0)
    t_pos = lax.broadcasted_iota(jnp.int32, (tokens, tokens), 1)

    def make_bucket():
        differ = jnp.bitwise_xor(s_pos, t_pos)
        bucket = jnp.zeros((tokens, tokens), jnp.int32)
        for exponent in range(local - 1):
            bucket = bucket + (differ >= 2**exponent).astype(jnp.int32)
        bucket_ref[...] = jnp.where(s_pos <= t_pos, bucket, -1)

    def near_forward(h):
        q_t = q_ref[h].T
        qt_ref[h] = q_t
        scores = dot(k_ref[h], q_t)
        scores_ref[h] = scores
        bucket = bucket_ref[...]
        weights = jnp.zeros((tokens, tokens), F32)
        for number in range(local):
            row = lw_ref[h, number : number + 1, :] * level_scale(number, dim)
            weights = jnp.where(bucket == number, row, weights)
        weights_ref[h] = weights
        weighted = (weights * scores).astype(BF16)
        weighted_ref[h] = weighted
        q_wide = q_t.astype(F32)
        for m in range(far):
            row = lw_ref[h, local + m : local + m + 1, :] * level_scale(local + m, dim)
            sq_ref[h, m * dim : (m + 1) * dim, :] = (row * q_wide).astype(BF16)
        att_ref[h] = dot(v_ref[h].T, weighted)
        gain = jnp.broadcast_to(gain_ref[h : h + 1, :], (tokens, dim))
        scaled_ref[h] = (gain * gn_ref[h].astype(F32)).T

    for h in range(per_chunk):
        key_value(h)
    pl.semaphore_wait(barrier, len(friends) + n_heads - 1)
    for c in range(chunks):
        if c > 0:
            for h in range(c * per_chunk, (c + 1) * per_chunk):
                key_value(h)
        fwd_copy(0, c).start()
    make_bucket()
    pending = list(range(heads))
    near_forward(pending.pop(0))
    for t in range(far + chunks - 1):
        for c in range(chunks):
            if 0 <= t - c < far:
                fwd_step(t - c, c)
        if pending:
            near_forward(pending.pop(0))
    while pending:
        near_forward(pending.pop(0))
    for m in range(far):

        @pl.when(bits[m] == 1)
        def _():
            for c in range(chunks):
                if m > 0:
                    local_wait(rcv.at[m], gather_rows(m), gar_sem.at[m, c])
            for h in range(heads):
                states_ref[h, m * dim : (m + 1) * dim, :] = rcv[m, h * dim : (h + 1) * dim, :].astype(BF16)

        @pl.when(bits[m] == 0)
        def _():
            for h in range(heads):
                states_ref[h, m * dim : (m + 1) * dim, :] = jnp.zeros((dim, dim), BF16)

    total = jnp.zeros((1, tokens), F32)
    inner = jnp.zeros((1, tokens), F32)
    for h in range(heads):
        att = att_ref[h] + dot(states_ref[h].T, sq_ref[h])
        att_ref[h] = att
        total = total + jnp.sum(att * att, axis=0, keepdims=True)
        inner = inner + jnp.sum(att * scaled_ref[h], axis=0, keepdims=True)
    hx[0:1, :] = total
    hx[1:2, :] = inner
    head_copies = [
        remote(hx, hx_in.at[j], hs_sem.at[j], hr_sem.at[j], (mine + j) % n_heads, "heads")
        for j in range(1, n_heads)
    ]
    for copy in head_copies:
        copy.start()
    for j, copy in enumerate(head_copies):
        copy.wait_recv()
        total = total + hx_in[j + 1, 0:1, :]
        inner = inner + hx_in[j + 1, 1:2, :]
    inv_rms = lax.rsqrt(total / width + EPS)
    pull = inv_rms * inv_rms * inv_rms * inner / width

    def scatter_copies(m, c):
        size = part >> m
        copies = []
        for j in range(1, 2**m):
            where = span(place(peer_bits(j), m, c), size)
            slot = pl.ds(j * chunks * size + c * size, size)
            copies.append(
                remote(gs.at[m, where, :], rs.at[m, slot, :], rss_sem.at[m, c], rsr_sem.at[m, c], peer(j))
            )
        return copies

    def up_copy(m, c):
        where = span(place(bits, m, c), part >> m)
        return remote(tx.at[m, where, :], brcv.at[m, where, :], bs_sem.at[m, c], br_sem.at[m, c], peer(2**m))

    def down_copy(m, c):
        where = span(place(bits[:m] + [0], m + 1, c), part >> (m + 1))
        return remote(
            abuf.at[m + 1, where, :], brcv.at[m, where, :], bs_sem.at[m, c], br_sem.at[m, c], peer(2**m)
        )

    def bwd_send(m, c):
        size = part >> m

        @pl.when(bits[m] == 1)
        def _():
            where = span(place(bits, m, c), size)
            sums = gs[m, where, :]
            if m > 0:
                local_wait(rs.at[m], gather_rows(m), rsr_sem.at[m, c])
                for j in range(1, 2**m):
                    slot = j * chunks * size + c * size
                    sums = sums + rs[m, slot : slot + size, :]
            tx[m, where, :] = sums
            if m < far - 1:
                half = span(place(bits[:m] + [1], m + 1, c), size // 2)
                tx[m, half, :] = tx[m, half, :] + abuf[m + 1, half, :]
            up_copy(m, c).start()

        if m < far - 1:

            @pl.when(bits[m] == 0)
            def _():
                down_copy(m, c).start()

    def bwd_recv(m, c):
        size = part >> m
        half0 = span(place(bits[:m] + [0], m + 1, c), size // 2)
        half1 = span(place(bits[:m] + [1], m + 1, c), size // 2)

        @pl.when(bits[m] == 0)
        def _():
            up_copy(m, c).wait_recv()
            low = brcv[m, half0, :]
            if m < far - 1:
                low = low + abuf[m + 1, half0, :]
            abuf[m, half0, :] = low
            abuf[m, half1, :] = brcv[m, half1, :]

        @pl.when(bits[m] == 1)
        def _():
            if m < far - 1:
                down_copy(m, c).wait_recv()
                abuf[m, half0, :] = brcv[m, half0, :]
                abuf[m, half1, :] = abuf[m + 1, half1, :]
            else:
                abuf[m, half0, :] = jnp.zeros((size // 2, dim), F32)
                abuf[m, half1, :] = jnp.zeros((size // 2, dim), F32)

    for c in range(chunks):
        for h in range(c * per_chunk, (c + 1) * per_chunk):
            g_t = (inv_rms * scaled_ref[h] - att_ref[h] * pull).astype(BF16)
            gt_ref[h] = g_t
            grads = dot_nt(sq_ref[h], g_t)
            for m in range(far):
                gs[m, h * dim : (h + 1) * dim, :] = grads[m * dim : (m + 1) * dim, :]
        for m in reversed(range(1, far)):

            @pl.when(bits[m] == 1)
            def _():
                for copy in scatter_copies(m, c):
                    copy.start()

    def near_backward(h):
        gain = jnp.broadcast_to(gain_ref[h : h + 1, :], (tokens, dim))
        normed_ref[h] = ((att_ref[h] * inv_rms).T * gain).astype(BF16)
        g_t = gt_ref[h]
        mix = dot(v_ref[h], g_t)
        grad_scores = (weights_ref[h] * mix).astype(BF16)
        product = mix * scores_ref[h]
        bucket = bucket_ref[...]
        for number in range(local):
            kept = jnp.where(bucket == number, product, 0.0)
            glw_ref[h, number : number + 1, :] = level_scale(number, dim) * jnp.sum(kept, axis=0, keepdims=True)
        grad_q = dot(k_ref[h].T, grad_scores)
        turned = dot(states_ref[h], g_t)
        q_wide = qt_ref[h].astype(F32)
        for m in range(far):
            block = turned[m * dim : (m + 1) * dim, :]
            scale = level_scale(local + m, dim)
            glw_ref[h, local + m : local + m + 1, :] = scale * jnp.sum(block * q_wide, axis=0, keepdims=True)
            grad_q = grad_q + (lw_ref[h, local + m : local + m + 1, :] * scale) * block
        gq_ref[h] = grad_q.T.astype(BF16)
        gk_acc[h] = dot_nt(grad_scores, qt_ref[h])
        gv_acc[h] = dot_nt(weighted_ref[h], g_t)

    pending = list(range(heads))
    near_backward(pending.pop(0))
    for t in range(far + chunks):
        for c in range(chunks):
            stage = t - c
            if 1 <= stage <= far:
                bwd_recv(far - stage, c)
                if stage == far:
                    for h in range(c * per_chunk, (c + 1) * per_chunk):
                        while h in pending:
                            near_backward(pending.pop(0))
                        grad_kv = abuf[0, h * dim : (h + 1) * dim, :].astype(BF16)
                        gk_ref[h] = (gk_acc[h] + dot_nt(v_ref[h], grad_kv)).astype(BF16)
                        gv_ref[h] = (gv_acc[h] + dot(k_ref[h], grad_kv)).astype(BF16)
            if 0 <= stage < far:
                bwd_send(far - 1 - stage, c)
        if pending:
            near_backward(pending.pop(0))

    for copy in head_copies:
        copy.wait_send()
    for c in range(chunks):
        for m in range(far):
            fwd_copy(m, c).wait_send()

            @pl.when(bits[m] == 1)
            def _():
                if m > 0:
                    local_wait(rcv.at[m], gather_rows(m), gas_sem.at[m, c])
                    local_wait(gs.at[m], gather_rows(m), rss_sem.at[m, c])
                up_copy(m, c).wait_send()

            if m < far - 1:

                @pl.when(bits[m] == 0)
                def _():
                    down_copy(m, c).wait_send()


def shards(n_ctx, n_heads, queries, key_rows, value_rows, level_weights, norm_gain, grad_normed):
    heads, tokens, dim = queries.shape
    far = n_ctx.bit_length() - 1
    rows = heads * dim
    chunks = max(c for c in (1, 2, 4) if heads % c == 0 and rows // c >> (far - 1) >= 16)
    vmem = pl.BlockSpec(memory_space=pltpu.VMEM)
    square = (heads, tokens, tokens)
    turned = (heads, dim, tokens)
    links = (far, rows, dim)
    dma = pltpu.SemaphoreType.DMA
    return pl.pallas_call(
        functools.partial(kernel, n_ctx, n_heads, chunks),
        out_shape=[jax.ShapeDtypeStruct(queries.shape, BF16)] * 4
        + [jax.ShapeDtypeStruct(level_weights.shape, F32)],
        in_specs=[vmem] * 6,
        out_specs=[vmem] * 5,
        scratch_shapes=[
            pltpu.VMEM((tokens, tokens), jnp.int32),
            pltpu.VMEM(turned, BF16),
            pltpu.VMEM(square, F32),
            pltpu.VMEM(square, F32),
            pltpu.VMEM(square, BF16),
            pltpu.VMEM((heads, far * dim, tokens), BF16),
            pltpu.VMEM(turned, F32),
            pltpu.VMEM(turned, F32),
            pltpu.VMEM(turned, BF16),
            pltpu.VMEM((heads, far * dim, dim), BF16),
            pltpu.VMEM(queries.shape, F32),
            pltpu.VMEM(queries.shape, F32),
        ]
        + [pltpu.VMEM(links, F32)] * 7
        + [pltpu.VMEM((8, tokens), F32), pltpu.VMEM((n_heads, 8, tokens), F32)]
        + [dma((far, chunks))] * 8
        + [dma((n_heads,))] * 2,
        compiler_params=pltpu.CompilerParams(
            collective_id=0, has_side_effects=True, vmem_limit_bytes=48 * 2**20
        ),
    )(queries, key_rows, value_rows, level_weights, norm_gain, grad_normed)


def solution(mesh):
    token_spec = P("heads", "ctx", None)
    in_specs = (token_spec,) * 3 + (P("heads", None, "ctx"), P("heads", None), token_spec)
    out_specs = (token_spec,) * 4 + (P("heads", None, "ctx"),)
    body = functools.partial(shards, mesh.shape["ctx"], mesh.shape["heads"])
    return jax.shard_map(body, mesh=mesh, in_specs=in_specs, out_specs=out_specs, check_vma=False)
```

time: 87.2 us -> 63 us (0.72)
  Pallas kernels: 0 us -> 53.9 us
  waiting for transfers between devices: 37.5 us -> 0 us
  starting transfers between devices: 16.6 us -> 0 us
  matrix products: 13.5 us -> 0 us
  other arithmetic: 7.87 us -> 0 us
  blocking collectives: 4.91 us -> 0 us
  local copies, waits for them, and re-layouts: 5.16 us -> 8.09 us
    pallas_call x0 -> x1, Pallas kernels: none -> 53.9 us  [shards(): pl.pallas_call(functools.partial(kernel, n_ctx, n_heads, chunks), out_sha...]
    ppermute x14 -> x0, waiting for transfers between devices: 37.5 us -> none  [from_partner(): return lax.ppermute(value, axis, pairs)]
    ppermute x14 -> x0, starting transfers between devices: 16.6 us -> none  [from_partner(): return lax.ppermute(value, axis, pairs)]
    dot_general x12 -> x0, matrix products: 13.5 us -> none  [the longest x1 2.28 us: shards(): jnp.einsum('hte,hse->hts', grad_out, value_rows, preferred_element_type=j...]
    unnamed x88 -> x15, local copies, waits for them, and re-layouts: 2.15 us -> 7.44 us
    psum x1 -> x0, blocking collectives: 4.91 us -> none  [shards(): totals = lax.psum(jnp.sum(attended * attended, axis=(0, 2)), 'heads')]
    add x4 -> x0, other arithmetic: 2.78 us -> none  [shards(): level_total = level_total + partner]
    reduce_sum x2 -> x0, other arithmetic: 2.32 us -> none  [the longest x1 1.42 us: shards(): jnp.sum(grad_wide * far_terms[depth], axis=2)]
  transfers between devices with their start and end apart: 14 -> 0, of which waited for: 10 -> 0; matrix products, arithmetic and copies ran while one was open for 14% -> 0% of each run, Pallas kernels for 0% -> 0%
where the time goes in v1:
time: 63 us; the launch traced here: 62.6 us
  Pallas kernels  53.9 us (86%)
  local copies, waits for them, and re-layouts  8.09 us (13%)
  between operations  0.67 us (1%)
    pallas_call x1, Pallas kernels, shards(): pl.pallas_call(functools.partial(kernel, n_ctx, n_heads, chunks), out_sha...  53.9 us
    unnamed x15, local copies, waits for them, and re-layouts  7.44 us

profile of v1, /device:TPU:0, one launch (start us, length us, event | category | flops | bytes accessed | tf_op | source)
XLA Modules:
  0.0 62.6 jit_solution(11732401221838892659)
XLA Ops:
  0.6 0.0 copy-start.4
  0.6 0.8 %copy.11.lw_ref = f32[4,13,256]{2,1,0:T(8,128)S(1)} copy(f32[4,13,256]{2,0,1:T(4,128)} %param.9) | data formatting | bytes 106496 | tf_op args[3]
  1.5 0.0 copy-done.4
  1.5 0.0 copy-start
  1.5 0.9 %copy-done = bf16[4,256,128]{2,1,0:T(8,128)(2,1)S(1)} copy-done((bf16[4,256,128]{2,1,0:T(8,128)(2,1)S(1)}, bf16[4,256,128]{2,1,0:T(8,128)(2,1)}, u32[]{:S(2)}) %copy-start) | copy-done | bytes 262168
  2.4 0.0 copy-start.1
  2.4 0.9 %copy-done.1 = bf16[4,256,128]{2,1,0:T(8,128)(2,1)S(1)} copy-done((bf16[4,256,128]{2,1,0:T(8,128)(2,1)S(1)}, bf16[4,256,128]{2,1,0:T(8,128)(2,1)}, u32[]{:S(2)}) %copy-start.1) | copy-done | bytes 262168
  3.4 0.0 copy-start.2
  3.4 0.9 %copy-done.2 = bf16[4,256,128]{2,1,0:T(8,128)(2,1)S(1)} copy-done((bf16[4,256,128]{2,1,0:T(8,128)(2,1)S(1)}, bf16[4,256,128]{2,1,0:T(8,128)(2,1)}, u32[]{:S(2)}) %copy-start.2) | copy-done | bytes 262168
  4.3 0.0 copy-start.3
  4.3 0.9 %copy-done.3 = bf16[4,256,128]{2,1,0:T(8,128)(2,1)S(1)} copy-done((bf16[4,256,128]{2,1,0:T(8,128)(2,1)S(1)}, bf16[4,256,128]{2,1,0:T(8,128)(2,1)}, u32[]{:S(2)}) %copy-start.3) | copy-done | bytes 262168
  5.3 53.9 %shard_map.101 = (bf16[4,256,128]{2,1,0:T(8,128)(2,1)S(1)}, bf16[4,256,128]{2,1,0:T(8,128)(2,1)S(1)}, bf16[4,256,128]{2,1,0:T(8,128)(2,1)S(1)}, bf16[4,256,128]{2,1,0:T(8,128)(2,1)S(1)}, f32[4,13,256]{2,1,0:T(8,128)S(1)}) custom-call(bf16[4,256,128]{2,1,0:T(8,128)(2,1)S(1)} %copy-done, bf16[4,256,128]{2,1,0:T(8,128)(2,1)S(1)} %copy-done.1, ...), custom_call_target="tpu_custom_call" | custom-call | tf_op jit(solution)/shard_map/pallas_call | solution.py:360
  59.1 0.7 %copy.12 = f32[4,13,256]{2,0,1:T(4,128)} copy(f32[4,13,256]{2,1,0:T(8,128)S(1)} %get-tuple-element.9) | data formatting | bytes 106496 | tf_op jit(solution)/shard_map/pallas_call | solution.py:360
  59.8 0.7 %copy.17 = bf16[4,256,128]{2,1,0:T(8,128)(2,1)} copy(bf16[4,256,128]{2,1,0:T(8,128)(2,1)S(1)} %get-tuple-element.15) | data formatting | bytes 524288
  60.5 0.7 %copy.18 = bf16[4,256,128]{2,1,0:T(8,128)(2,1)} copy(bf16[4,256,128]{2,1,0:T(8,128)(2,1)S(1)} %get-tuple-element.16) | data formatting | bytes 524288
  61.2 0.7 %copy.19 = bf16[4,256,128]{2,1,0:T(8,128)(2,1)} copy(bf16[4,256,128]{2,1,0:T(8,128)(2,1)S(1)} %get-tuple-element.17) | data formatting | bytes 524288
  61.9 0.7 %copy.20 = bf16[4,256,128]{2,1,0:T(8,128)(2,1)} copy(bf16[4,256,128]{2,1,0:T(8,128)(2,1)S(1)} %get-tuple-element.18) | data formatting | bytes 524288
Async XLA Ops:
  0.6 0.8 %copy-start.4 = (f32[4,128]{1,0:T(4,128)S(1)}, f32[4,128]{1,0:T(4,128)}, u32[]{:S(2)}) copy-start(f32[4,128]{1,0:T(4,128)} %gain_ref.1) | copy-start | bytes 6148
  1.5 1.0 %copy-start = (bf16[4,256,128]{2,1,0:T(8,128)(2,1)S(1)}, bf16[4,256,128]{2,1,0:T(8,128)(2,1)}, u32[]{:S(2)}) copy-start(bf16[4,256,128]{2,1,0:T(8,128)(2,1)} %q_ref.1) | copy-start | bytes 786436
  2.4 0.9 %copy-start.1 = (bf16[4,256,128]{2,1,0:T(8,128)(2,1)S(1)}, bf16[4,256,128]{2,1,0:T(8,128)(2,1)}, u32[]{:S(2)}) copy-start(bf16[4,256,128]{2,1,0:T(8,128)(2,1)} %k_ref.1) | copy-start | bytes 786436
  3.4 0.9 %copy-start.2 = (bf16[4,256,128]{2,1,0:T(8,128)(2,1)S(1)}, bf16[4,256,128]{2,1,0:T(8,128)(2,1)}, u32[]{:S(2)}) copy-start(bf16[4,256,128]{2,1,0:T(8,128)(2,1)} %v_ref.1) | copy-start | bytes 786436
  4.3 0.9 %copy-start.3 = (bf16[4,256,128]{2,1,0:T(8,128)(2,1)S(1)}, bf16[4,256,128]{2,1,0:T(8,128)(2,1)}, u32[]{:S(2)}) copy-start(bf16[4,256,128]{2,1,0:T(8,128)(2,1)} %gn_ref.1) | copy-start | bytes 786436

commit v2 on v1

--- a/solution.py
+++ b/solution.py
@@ -28,8 +28,9 @@
 
 def kernel(
     n_ctx, n_heads, chunks,
-    q_ref, k_ref, v_ref, lw_ref, gain_ref, gn_ref,
+    q_in, k_in, v_in, lw_in, gain_in, gn_in,
     normed_ref, gq_ref, gk_ref, gv_ref, glw_ref,
+    q_ref, k_ref, v_ref, lw_ref, gain_ref, gn_ref, in_sem,
     bucket_ref, qt_ref, scores_ref, weights_ref, weighted_ref, sq_ref, att_ref, scaled_ref, gt_ref,
     states_ref, gk_acc, gv_acc,
     gsum, rcv, gs, rs, tx, brcv, abuf, hx, hx_in,
@@ -65,6 +66,11 @@
     def span(start, size):
         return pl.ds(pl.multiple_of(start, 8), size)
 
+    pairs = ((k_in, k_ref), (v_in, v_ref), (q_in, q_ref), (lw_in, lw_ref), (gain_in, gain_ref), (gn_in, gn_ref))
+    loads = [pltpu.make_async_copy(src, dst, in_sem.at[i]) for i, (src, dst) in enumerate(pairs)]
+    for load in loads:
+        load.start()
+
     barrier = pltpu.get_barrier_semaphore()
     friends = list(range(1, n_ctx // 2)) + [n_ctx // 2]
     for j in friends:
@@ -133,19 +139,21 @@
         bucket = bucket_ref[...]
         weights = jnp.zeros((tokens, tokens), F32)
         for number in range(local):
-            row = lw_ref[h, number : number + 1, :] * level_scale(number, dim)
+            row = lw_ref[number, h : h + 1, :] * level_scale(number, dim)
             weights = jnp.where(bucket == number, row, weights)
         weights_ref[h] = weights
         weighted = (weights * scores).astype(BF16)
         weighted_ref[h] = weighted
         q_wide = q_t.astype(F32)
         for m in range(far):
-            row = lw_ref[h, local + m : local + m + 1, :] * level_scale(local + m, dim)
+            row = lw_ref[local + m, h : h + 1, :] * level_scale(local + m, dim)
             sq_ref[h, m * dim : (m + 1) * dim, :] = (row * q_wide).astype(BF16)
         att_ref[h] = dot(v_ref[h].T, weighted)
         gain = jnp.broadcast_to(gain_ref[h : h + 1, :], (tokens, dim))
         scaled_ref[h] = (gain * gn_ref[h].astype(F32)).T
 
+    loads[0].wait()
+    loads[1].wait()
     for h in range(per_chunk):
         key_value(h)
     pl.semaphore_wait(barrier, len(friends) + n_heads - 1)
@@ -155,6 +163,8 @@
                 key_value(h)
         fwd_copy(0, c).start()
     make_bucket()
+    for load in loads[2:]:
+        load.wait()
     pending = list(range(heads))
     near_forward(pending.pop(0))
     for t in range(far + chunks - 1):
@@ -295,15 +305,15 @@
         bucket = bucket_ref[...]
         for number in range(local):
             kept = jnp.where(bucket == number, product, 0.0)
-            glw_ref[h, number : number + 1, :] = level_scale(number, dim) * jnp.sum(kept, axis=0, keepdims=True)
+            glw_ref[number, h : h + 1, :] = level_scale(number, dim) * jnp.sum(kept, axis=0, keepdims=True)
         grad_q = dot(k_ref[h].T, grad_scores)
         turned = dot(states_ref[h], g_t)
         q_wide = qt_ref[h].astype(F32)
         for m in range(far):
             block = turned[m * dim : (m + 1) * dim, :]
             scale = level_scale(local + m, dim)
-            glw_ref[h, local + m : local + m + 1, :] = scale * jnp.sum(block * q_wide, axis=0, keepdims=True)
-            grad_q = grad_q + (lw_ref[h, local + m : local + m + 1, :] * scale) * block
+            glw_ref[local + m, h : h + 1, :] = scale * jnp.sum(block * q_wide, axis=0, keepdims=True)
+            grad_q = grad_q + (lw_ref[local + m, h : h + 1, :] * scale) * block
         gq_ref[h] = grad_q.T.astype(BF16)
         gk_acc[h] = dot_nt(grad_scores, qt_ref[h])
         gv_acc[h] = dot_nt(weighted_ref[h], g_t)
@@ -347,23 +357,39 @@
                     down_copy(m, c).wait_send()
 
 
+def put_out(*refs):
+    copies = [pltpu.make_async_copy(refs[i], refs[5 + i], refs[10].at[i]) for i in range(5)]
+    for copy in copies:
+        copy.start()
+    for copy in copies:
+        copy.wait()
+
+
 def shards(n_ctx, n_heads, queries, key_rows, value_rows, level_weights, norm_gain, grad_normed):
     heads, tokens, dim = queries.shape
     far = n_ctx.bit_length() - 1
     rows = heads * dim
-    chunks = max(c for c in (1, 2, 4) if heads % c == 0 and rows // c >> (far - 1) >= 16)
+    chunks = 1
     vmem = pl.BlockSpec(memory_space=pltpu.VMEM)
     square = (heads, tokens, tokens)
     turned = (heads, dim, tokens)
     links = (far, rows, dim)
     dma = pltpu.SemaphoreType.DMA
-    return pl.pallas_call(
+    rates = jnp.transpose(level_weights, (1, 0, 2))
+    results = pl.pallas_call(
         functools.partial(kernel, n_ctx, n_heads, chunks),
         out_shape=[jax.ShapeDtypeStruct(queries.shape, BF16)] * 4
-        + [jax.ShapeDtypeStruct(level_weights.shape, F32)],
-        in_specs=[vmem] * 6,
+        + [jax.ShapeDtypeStruct(rates.shape, F32)],
+        in_specs=[pl.BlockSpec(memory_space=pltpu.HBM)] * 6,
         out_specs=[vmem] * 5,
         scratch_shapes=[
+            pltpu.VMEM(queries.shape, BF16),
+            pltpu.VMEM(queries.shape, BF16),
+            pltpu.VMEM(queries.shape, BF16),
+            pltpu.VMEM(rates.shape, F32),
+            pltpu.VMEM(norm_gain.shape, F32),
+            pltpu.VMEM(queries.shape, BF16),
+            dma((6,)),
             pltpu.VMEM((tokens, tokens), jnp.int32),
             pltpu.VMEM(turned, BF16),
             pltpu.VMEM(square, F32),
@@ -384,7 +410,16 @@
         compiler_params=pltpu.CompilerParams(
             collective_id=0, has_side_effects=True, vmem_limit_bytes=48 * 2**20
         ),
-    )(queries, key_rows, value_rows, level_weights, norm_gain, grad_normed)
+    )(queries, key_rows, value_rows, rates, norm_gain, grad_normed)
+    results = pl.pallas_call(
+        put_out,
+        out_shape=[jax.ShapeDtypeStruct(x.shape, x.dtype) for x in results],
+        in_specs=[pl.BlockSpec(memory_space=pl.ANY)] * 5,
+        out_specs=[pl.BlockSpec(memory_space=pltpu.HBM)] * 5,
+        scratch_shapes=[dma((5,))],
+        compiler_params=pltpu.CompilerParams(vmem_limit_bytes=2**20),
+    )(*results)
+    return (*results[:4], jnp.transpose(results[4], (1, 0, 2)))
 
 
 def solution(mesh):

time: 63 us -> 49.6 us (0.79)
  Pallas kernels: 53.9 us -> 43.1 us
  local copies, waits for them, and re-layouts: 8.09 us -> 5.28 us
    pallas_call x1, Pallas kernels: 53.9 us -> 42.1 us  [shards(): pl.pallas_call(functools.partial(kernel, n_ctx, n_heads, chunks), out_sha...]
    unnamed x15 -> x12, local copies, waits for them, and re-layouts: 7.44 us -> 5.28 us
    pallas_call x0 -> x1, Pallas kernels: none -> 1.01 us  [shards(): pl.pallas_call(put_out, out_shape=[jax.ShapeDtypeStruct(x.shape, x.dtype)...]
    pallas_call x1 -> x0, local copies, waits for them, and re-layouts: 0.66 us -> none  [shards(): pl.pallas_call(functools.partial(kernel, n_ctx, n_heads, chunks), out_sha...]
where the time goes in v2:
time: 49.6 us; the launch traced here: 49 us
  Pallas kernels  43.1 us (87%)
  local copies, waits for them, and re-layouts  5.28 us (11%)
  between operations  0.65 us (1%)
    pallas_call x1, Pallas kernels, shards(): pl.pallas_call(functools.partial(kernel, n_ctx, n_heads, chunks), out_sha...  42.1 us
    unnamed x12, local copies, waits for them, and re-layouts  5.28 us
    pallas_call x1, Pallas kernels, shards(): pl.pallas_call(put_out, out_shape=[jax.ShapeDtypeStruct(x.shape, x.dtype)...  1.01 us

profile of v2, /device:TPU:0, one launch (start us, length us, event | category | flops | bytes accessed | tf_op | source)
XLA Modules:
  0.0 49.0 jit_solution(6762648641225948806)
XLA Ops:
  0.6 0.0 copy-start
  0.6 0.9 %copy-done = bf16[4,256,128]{2,1,0:T(8,128)(2,1)S(1)} copy-done((bf16[4,256,128]{2,1,0:T(8,128)(2,1)S(1)}, bf16[4,256,128]{2,1,0:T(8,128)(2,1)}, u32[]{:S(2)}) %copy-start) | copy-done | bytes 262168
  1.6 0.0 copy-start.1
  1.6 0.9 %copy-done.1 = bf16[4,256,128]{2,1,0:T(8,128)(2,1)S(1)} copy-done((bf16[4,256,128]{2,1,0:T(8,128)(2,1)S(1)}, bf16[4,256,128]{2,1,0:T(8,128)(2,1)}, u32[]{:S(2)}) %copy-start.1) | copy-done | bytes 262168
  2.5 0.0 copy-start.2
  2.5 0.9 %copy-done.2 = bf16[4,256,128]{2,1,0:T(8,128)(2,1)S(1)} copy-done((bf16[4,256,128]{2,1,0:T(8,128)(2,1)S(1)}, bf16[4,256,128]{2,1,0:T(8,128)(2,1)}, u32[]{:S(2)}) %copy-start.2) | copy-done | bytes 262168
  3.5 0.0 copy-start.3
  3.5 0.9 %copy-done.3 = bf16[4,256,128]{2,1,0:T(8,128)(2,1)S(1)} copy-done((bf16[4,256,128]{2,1,0:T(8,128)(2,1)S(1)}, bf16[4,256,128]{2,1,0:T(8,128)(2,1)}, u32[]{:S(2)}) %copy-start.3) | copy-done | bytes 262168
  4.4 0.0 copy-start.4
  4.4 0.8 %copy-done.4 = f32[4,13,256]{2,0,1:T(4,128)S(1)} copy-done((f32[4,13,256]{2,0,1:T(4,128)S(1)}, f32[4,13,256]{2,0,1:T(4,128)}, u32[]{:S(2)}) %copy-start.4) | copy-done | bytes 53272
  5.2 0.0 copy-start.5
  5.2 0.7 %copy-done.5 = f32[4,128]{1,0:T(4,128)S(1)} copy-done((f32[4,128]{1,0:T(4,128)S(1)}, f32[4,128]{1,0:T(4,128)}, u32[]{:S(2)}) %copy-start.5) | copy-done | bytes 2072
  5.9 42.1 %shard_map.101 = (bf16[4,256,128]{2,1,0:T(8,128)(2,1)S(1)}, bf16[4,256,128]{2,1,0:T(8,128)(2,1)S(1)}, bf16[4,256,128]{2,1,0:T(8,128)(2,1)S(1)}, bf16[4,256,128]{2,1,0:T(8,128)(2,1)S(1)}, f32[13,4,256]{2,1,0:T(4,128)S(1)}) custom-call(bf16[4,256,128]{2,1,0:T(8,128)(2,1)S(1)} %copy-done, bf16[4,256,128]{2,1,0:T(8,128)(2,1)S(1)} %copy-done.1, ...), custom_call_target="tpu_custom_call" | custom-call | tf_op jit(solution)/shard_map/pallas_call | solution.py:379
  48.0 1.0 %shard_map.102 = (bf16[4,256,128]{2,1,0:T(8,128)(2,1)}, bf16[4,256,128]{2,1,0:T(8,128)(2,1)}, bf16[4,256,128]{2,1,0:T(8,128)(2,1)}, bf16[4,256,128]{2,1,0:T(8,128)(2,1)}, f32[13,4,256]{2,1,0:T(4,128)}) custom-call(bf16[4,256,128]{2,1,0:T(8,128)(2,1)S(1)} %get-tuple-element.15.refs_0_, bf16[4,256,128]{2,1,0:T(8,128)(2,1)S(1)} %get-tuple-element.16.refs_1_, ...), custom_call_target="tpu_custom_call" | custom-call | tf_op jit(solution)/shard_map/pallas_call | solution.py:414
Async XLA Ops:
  0.6 1.0 %copy-start = (bf16[4,256,128]{2,1,0:T(8,128)(2,1)S(1)}, bf16[4,256,128]{2,1,0:T(8,128)(2,1)}, u32[]{:S(2)}) copy-start(bf16[4,256,128]{2,1,0:T(8,128)(2,1)} %q_in.1) | copy-start | bytes 786436
  1.6 0.9 %copy-start.1 = (bf16[4,256,128]{2,1,0:T(8,128)(2,1)S(1)}, bf16[4,256,128]{2,1,0:T(8,128)(2,1)}, u32[]{:S(2)}) copy-start(bf16[4,256,128]{2,1,0:T(8,128)(2,1)} %k_in.1) | copy-start | bytes 786436
  2.5 0.9 %copy-start.2 = (bf16[4,256,128]{2,1,0:T(8,128)(2,1)S(1)}, bf16[4,256,128]{2,1,0:T(8,128)(2,1)}, u32[]{:S(2)}) copy-start(bf16[4,256,128]{2,1,0:T(8,128)(2,1)} %v_in.1) | copy-start | bytes 786436
  3.5 0.9 %copy-start.3 = (bf16[4,256,128]{2,1,0:T(8,128)(2,1)S(1)}, bf16[4,256,128]{2,1,0:T(8,128)(2,1)}, u32[]{:S(2)}) copy-start(bf16[4,256,128]{2,1,0:T(8,128)(2,1)} %gn_in.1) | copy-start | bytes 786436
  4.4 0.8 %copy-start.4 = (f32[4,13,256]{2,0,1:T(4,128)S(1)}, f32[4,13,256]{2,0,1:T(4,128)}, u32[]{:S(2)}) copy-start(f32[4,13,256]{2,0,1:T(4,128)} %param.9) | copy-start | bytes 159748
  5.2 0.7 %copy-start.5 = (f32[4,128]{1,0:T(4,128)S(1)}, f32[4,128]{1,0:T(4,128)}, u32[]{:S(2)}) copy-start(f32[4,128]{1,0:T(4,128)} %gain_in.1) | copy-start | bytes 6148

commit v3 on v2

--- a/solution.py
+++ b/solution.py
@@ -410,7 +410,7 @@
         compiler_params=pltpu.CompilerParams(
             collective_id=0, has_side_effects=True, vmem_limit_bytes=48 * 2**20
         ),
-    )(queries, key_rows, value_rows, rates, norm_gain, grad_normed)
+    )(*[pltpu.with_memory_space_constraint(x, pltpu.HBM) for x in (queries, key_rows, value_rows, rates, norm_gain, grad_normed)])
     results = pl.pallas_call(
         put_out,
         out_shape=[jax.ShapeDtypeStruct(x.shape, x.dtype) for x in results],

time: 49.6 us -> 44 us (0.89)
  local copies, waits for them, and re-layouts: 5.28 us -> 0 us
    unnamed x12 -> x0, local copies, waits for them, and re-layouts: 5.28 us -> none
where the time goes in v3:
time: 44 us; the launch traced here: 43.6 us
  Pallas kernels  43 us (98%)
  between operations  0.64 us (1%)
    pallas_call x1, Pallas kernels, shards(): pl.pallas_call(functools.partial(kernel, n_ctx, n_heads, chunks), out_sha...  42 us
    pallas_call x1, Pallas kernels, shards(): pl.pallas_call(put_out, out_shape=[jax.ShapeDtypeStruct(x.shape, x.dtype)...  1.01 us

profile of v3, /device:TPU:0, one launch (start us, length us, event | category | flops | bytes accessed | tf_op | source)
XLA Modules:
  0.0 43.6 jit_solution(17551749019657463739)
XLA Ops:
  0.6 42.0 %shard_map.101 = (bf16[4,256,128]{2,1,0:T(8,128)(2,1)S(1)}, bf16[4,256,128]{2,1,0:T(8,128)(2,1)S(1)}, bf16[4,256,128]{2,1,0:T(8,128)(2,1)S(1)}, bf16[4,256,128]{2,1,0:T(8,128)(2,1)S(1)}, f32[13,4,256]{2,1,0:T(4,128)S(1)}) custom-call(bf16[4,256,128]{2,1,0:T(8,128)(2,1)} %q_in.1, bf16[4,256,128]{2,1,0:T(8,128)(2,1)} %k_in.1, bf16[4,256,128]{2,1,0:T(8,128)(2,1)} %v_in.1, ...), custom_call_target="tpu_custom_call" | custom-call | tf_op jit(solution)/shard_map/pallas_call | solution.py:379
  42.6 1.0 %shard_map.102 = (bf16[4,256,128]{2,1,0:T(8,128)(2,1)}, bf16[4,256,128]{2,1,0:T(8,128)(2,1)}, bf16[4,256,128]{2,1,0:T(8,128)(2,1)}, bf16[4,256,128]{2,1,0:T(8,128)(2,1)}, f32[13,4,256]{2,1,0:T(4,128)}) custom-call(bf16[4,256,128]{2,1,0:T(8,128)(2,1)S(1)} %get-tuple-element.15.refs_0_, bf16[4,256,128]{2,1,0:T(8,128)(2,1)S(1)} %get-tuple-element.16.refs_1_, ...), custom_call_target="tpu_custom_call" | custom-call | tf_op jit(solution)/shard_map/pallas_call | solution.py:414

commit v4 on v3

--- a/solution.py
+++ b/solution.py
@@ -166,7 +166,6 @@
     for load in loads[2:]:
         load.wait()
     pending = list(range(heads))
-    near_forward(pending.pop(0))
     for t in range(far + chunks - 1):
         for c in range(chunks):
             if 0 <= t - c < far:

time: 44 us -> 44 us (level)
  no operation moved by 1% of the time
where the time goes in v4:
time: 44 us; the launch traced here: 43.6 us
  Pallas kernels  43 us (98%)
  between operations  0.64 us (1%)
    pallas_call x1, Pallas kernels, shards(): pl.pallas_call(functools.partial(kernel, n_ctx, n_heads, chunks), out_sha...  42 us
    pallas_call x1, Pallas kernels, shards(): pl.pallas_call(put_out, out_shape=[jax.ShapeDtypeStruct(x.shape, x.dtype)...  1.01 us

profile of v4, /device:TPU:0, one launch (start us, length us, event | category | flops | bytes accessed | tf_op | source)
XLA Modules:
  0.0 43.6 jit_solution(6415277719462479746)
XLA Ops:
  0.6 42.0 %shard_map.101 = (bf16[4,256,128]{2,1,0:T(8,128)(2,1)S(1)}, bf16[4,256,128]{2,1,0:T(8,128)(2,1)S(1)}, bf16[4,256,128]{2,1,0:T(8,128)(2,1)S(1)}, bf16[4,256,128]{2,1,0:T(8,128)(2,1)S(1)}, f32[13,4,256]{2,1,0:T(4,128)S(1)}) custom-call(bf16[4,256,128]{2,1,0:T(8,128)(2,1)} %q_in.1, bf16[4,256,128]{2,1,0:T(8,128)(2,1)} %k_in.1, bf16[4,256,128]{2,1,0:T(8,128)(2,1)} %v_in.1, ...), custom_call_target="tpu_custom_call" | custom-call | tf_op jit(solution)/shard_map/pallas_call | solution.py:378
  42.6 1.0 %shard_map.102 = (bf16[4,256,128]{2,1,0:T(8,128)(2,1)}, bf16[4,256,128]{2,1,0:T(8,128)(2,1)}, bf16[4,256,128]{2,1,0:T(8,128)(2,1)}, bf16[4,256,128]{2,1,0:T(8,128)(2,1)}, f32[13,4,256]{2,1,0:T(4,128)}) custom-call(bf16[4,256,128]{2,1,0:T(8,128)(2,1)S(1)} %get-tuple-element.15.refs_0_, bf16[4,256,128]{2,1,0:T(8,128)(2,1)S(1)} %get-tuple-element.16.refs_1_, ...), custom_call_target="tpu_custom_call" | custom-call | tf_op jit(solution)/shard_map/pallas_call | solution.py:413
